TPU v7x, 512 devices: a whole 4x8x8 slice. The times are simulated.
512 devices in a mesh: dp: 2 (over core), ctx: 64 (over z, y), head: 4 (over x).
Axes of the slice: x: 4, y: 8, z: 8, core: 2. Of those that a mesh axis runs over, the one named last changes fastest.
Arguments:
- queries: bfloat16 [2, 8192, 2560], P('dp', 'ctx', 'head'), may hold values from -25 to 25
- keys: bfloat16 [2, 8192, 2560], P('dp', 'ctx', 'head'), may hold values from -25 to 25
- values: bfloat16 [2, 8192, 2560], P('dp', 'ctx', 'head'), may hold values from -6 to 6
- grad_y: bfloat16 [2, 8192, 2560], P('dp', 'ctx', 'head'), may hold values from -6 to 6
- out_gain: float32 [2560], P('head'), may hold values from 0.1 to 1.9
- offsets: int32 [2, 20], P(None, 'head'), may hold values from 0 to 63, as said below
Outputs:
- attended: bfloat16 [2, 8192, 2560], P('dp', 'ctx', 'head')
- query_grad: bfloat16 [2, 8192, 2560], P('dp', 'ctx', 'head')
- key_grad: bfloat16 [2, 8192, 2560], P('dp', 'ctx', 'head')
- value_grad: bfloat16 [2, 8192, 2560], P('dp', 'ctx', 'head')
- gain_grad: float32 [2560], P('head')
Inputs may be any that keep to these rules, and one draw needn't show every extreme that they name: Row 0 holds offsets below 8, row 1 offsets below 64.
All inputs are finite; a program needn't handle non-finite values.
Results may differ from a plain program's by a relative error of at most 0.011.
Values may be sent and summed in bfloat16 or wider, within the bound.
A program may use at most 64 MiB of HBM per device.

v0:
```python
import math
import jax
import jax.numpy as jnp
from jax import lax
from jax.sharding import PartitionSpec as P

HEAD_DIM = 128
SPAN = 4
R1 = 8
EPS = 1e-06


def group_gather(block, axis, group):
    count = lax.axis_size(axis)
    pieces = [block]
    for shift in range(1, group):
        route = []
        for src in range(count):
            base = src - src % group
            route.append((src, base + (src % group + shift) % group))
        pieces.append(lax.ppermute(block, axis, route))
    return jnp.concatenate(pieces, 0)


def pick_rows(source_rows, dilation, shifts):
    row_count, head_count, head_width = source_rows.shape
    grouped = source_rows.reshape(row_count // dilation, dilation, head_count, head_width)
    hit_mask = jnp.arange(dilation, dtype=jnp.int32).reshape(1, dilation, 1, 1) == shifts.reshape(
        1, 1, head_count, 1
    )
    chosen = jnp.where(hit_mask, grouped, jnp.zeros((), source_rows.dtype))
    return jnp.sum(chosen, axis=1, dtype=source_rows.dtype)


def place_rows(row_values, dilation, shifts):
    row_count, head_count, head_width = row_values.shape
    hit_mask = jnp.arange(dilation, dtype=jnp.int32).reshape(1, dilation, 1, 1) == shifts.reshape(
        1, 1, head_count, 1
    )
    spread = jnp.where(hit_mask, row_values[:, None], jnp.zeros((), row_values.dtype))
    return spread.reshape(row_count * dilation, head_count, head_width)


def level_scores(q_rows, k_rows):
    score_scale = 1.0 / math.sqrt(q_rows.shape[-1])
    return (
        jnp.einsum("qhe,khe->hqk", q_rows, k_rows, preferred_element_type=jnp.float32) * score_scale
    )


def attend(q_rows, k_rows, v_rows):
    scores = level_scores(q_rows, k_rows)
    row_max = jnp.max(scores, axis=-1, keepdims=True)
    log_total = row_max[..., 0] + jnp.log(jnp.sum(jnp.exp(scores - row_max), axis=-1))
    soft_rows = jnp.exp(scores - log_total[..., None]).astype(jnp.bfloat16)
    level_out = jnp.einsum("hqk,khe->qhe", soft_rows, v_rows, preferred_element_type=jnp.float32)
    return (level_out, log_total.T)


def score_grads(q_rows, k_rows, v_rows, log_total, grad_low, row_shift):
    score_scale = 1.0 / math.sqrt(q_rows.shape[-1])
    scores = level_scores(q_rows, k_rows)
    exact_soft = jnp.exp(scores - log_total.T[..., None])
    prob_grad = jnp.einsum("qhe,khe->hqk", grad_low, v_rows, preferred_element_type=jnp.float32)
    score_grad = (exact_soft * (prob_grad + row_shift.T[..., None]) * score_scale).astype(
        jnp.bfloat16
    )
    return (score_grad, exact_soft.astype(jnp.bfloat16))


def key_parts(score_grad, soft_low, q_rows, grad_low):
    k_part = jnp.einsum("hqk,qhe->khe", score_grad, q_rows, preferred_element_type=jnp.float32)
    v_part = jnp.einsum("hqk,qhe->khe", soft_low, grad_low, preferred_element_type=jnp.float32)
    return (k_part, v_part)


def query_part(score_grad, k_rows):
    return jnp.einsum("hqk,khe->qhe", score_grad, k_rows, preferred_element_type=jnp.float32)


def split_qkv(packed, head_count):
    width = head_count * HEAD_DIM
    shape = (packed.shape[0], head_count, HEAD_DIM)
    return tuple((packed[:, i * width : (i + 1) * width].reshape(shape) for i in range(3)))


def pack_grads(grad_low, row_shift):
    rows = grad_low.shape[0]
    return jnp.concatenate(
        [grad_low.astype(jnp.float32).reshape(rows, -1), row_shift.astype(jnp.float32)], 1
    )


def unpack_grads(packed, head_count):
    width = head_count * HEAD_DIM
    grad_low = packed[:, :width].astype(jnp.bfloat16).reshape(-1, head_count, HEAD_DIM)
    return (grad_low, packed[:, width:])


def shards(queries, keys, values, grad_y, out_gain, offsets):
    tokens = queries.shape[1]
    flat_width = queries.shape[2]
    head_count = flat_width // HEAD_DIM
    row_shape = (tokens, head_count, HEAD_DIM)
    q_own = queries[0].reshape(row_shape)
    k_own = keys[0].reshape(row_shape)
    v_own = values[0].reshape(row_shape)
    ctx_size = lax.axis_size("ctx")
    my_place = lax.axis_index("ctx")
    mid_shift = offsets[0]
    top_shift = offsets[1]
    positions = jnp.arange(tokens, dtype=jnp.int32)
    mid_hit = (positions % R1)[:, None] == mid_shift[None, :]
    top_hit = (positions % ctx_size)[:, None] == top_shift[None, :]
    mid_pack = jnp.concatenate(
        [pick_rows(x, R1, mid_shift).reshape(-1, flat_width) for x in (q_own, k_own, v_own)], 1
    )
    top_pack = jnp.concatenate(
        [pick_rows(x, ctx_size, top_shift).reshape(-1, flat_width) for x in (q_own, k_own, v_own)],
        1,
    )
    mid_rows = mid_pack.shape[0]
    top_rows = top_pack.shape[0]
    mid_all = group_gather(mid_pack, "ctx", SPAN)
    top_all = lax.all_gather(top_pack, "ctx", axis=0, tiled=True)
    mid_q, mid_k, mid_v = split_qkv(mid_all, head_count)
    top_q, top_k, top_v = split_qkv(top_all, head_count)
    top_start = my_place * top_rows
    base_out, base_total = attend(q_own, k_own, v_own)
    mid_out_all, mid_total_all = attend(mid_q, mid_k, mid_v)
    top_out_all, top_total_all = attend(top_q, top_k, top_v)
    mid_out = mid_out_all[:mid_rows]
    mid_total = mid_total_all[:mid_rows]
    top_out = lax.dynamic_slice_in_dim(top_out_all, top_start, top_rows, 0)
    top_total = lax.dynamic_slice_in_dim(top_total_all, top_start, top_rows, 0)
    mid_full = place_rows(mid_total[..., None], R1, mid_shift)[..., 0]
    top_full = place_rows(top_total[..., None], ctx_size, top_shift)[..., 0]
    row_max = jnp.maximum(base_total, jnp.where(mid_hit, mid_full, base_total))
    row_max = jnp.maximum(row_max, jnp.where(top_hit, top_full, base_total))
    base_expo = jnp.exp(base_total - row_max)
    mid_expo = jnp.where(mid_hit, jnp.exp(mid_full - row_max), 0.0)
    top_expo = jnp.where(top_hit, jnp.exp(top_full - row_max), 0.0)
    denom = base_expo + mid_expo + top_expo
    base_share = base_expo / denom
    mid_share = mid_expo / denom
    top_share = top_expo / denom
    attn = (
        base_share[..., None] * base_out
        + mid_share[..., None] * place_rows(mid_out, R1, mid_shift)
        + top_share[..., None] * place_rows(top_out, ctx_size, top_shift)
    )
    inv_rms = lax.rsqrt(jnp.mean(attn * attn, axis=-1, keepdims=True) + EPS)
    normed = attn * inv_rms
    gain_rows = out_gain.reshape(head_count, HEAD_DIM)
    attended = (normed * gain_rows).astype(jnp.bfloat16).reshape(1, tokens, flat_width)
    grad_full = grad_y[0].reshape(row_shape).astype(jnp.float32)
    gain_part = jnp.sum(grad_full * normed, axis=0).reshape(flat_width)
    gain_grad = lax.psum(gain_part, ("dp", "ctx"))
    grad_norm = grad_full * gain_rows
    grad_attn = inv_rms * (
        grad_norm - normed * jnp.mean(grad_norm * normed, axis=-1, keepdims=True)
    )
    inner = jnp.sum(grad_attn * attn, axis=-1)
    base_low = (base_share[..., None] * grad_attn).astype(jnp.bfloat16)
    base_shift = -(base_share * inner)
    base_grad, base_soft = score_grads(q_own, k_own, v_own, base_total, base_low, base_shift)
    base_dq = query_part(base_grad, k_own)
    base_dk, base_dv = key_parts(base_grad, base_soft, q_own, base_low)
    mid_sel = pick_rows(mid_share[..., None], R1, mid_shift)[..., 0]
    mid_low = (mid_sel[..., None] * pick_rows(grad_attn, R1, mid_shift)).astype(jnp.bfloat16)
    mid_row_shift = -(mid_sel * pick_rows(inner[..., None], R1, mid_shift)[..., 0])
    top_sel = pick_rows(top_share[..., None], ctx_size, top_shift)[..., 0]
    top_low = (top_sel[..., None] * pick_rows(grad_attn, ctx_size, top_shift)).astype(jnp.bfloat16)
    top_row_shift = -(top_sel * pick_rows(inner[..., None], ctx_size, top_shift)[..., 0])
    mid_low_all, mid_shift_all = unpack_grads(
        group_gather(pack_grads(mid_low, mid_row_shift), "ctx", SPAN), head_count
    )
    top_low_all, top_shift_all = unpack_grads(
        lax.all_gather(pack_grads(top_low, top_row_shift), "ctx", axis=0, tiled=True), head_count
    )
    mid_grad, mid_soft = score_grads(mid_q, mid_k, mid_v, mid_total_all, mid_low_all, mid_shift_all)
    mid_dq = query_part(mid_grad[:, :mid_rows], mid_k)
    mid_dk, mid_dv = key_parts(
        mid_grad[:, :, :mid_rows], mid_soft[:, :, :mid_rows], mid_q, mid_low_all
    )
    top_grad, top_soft = score_grads(top_q, top_k, top_v, top_total_all, top_low_all, top_shift_all)
    own_grad = lax.dynamic_slice_in_dim(top_grad, top_start, top_rows, 1)
    top_dq = query_part(own_grad, top_k)
    key_grad_cols = lax.dynamic_slice_in_dim(top_grad, top_start, top_rows, 2)
    key_soft_cols = lax.dynamic_slice_in_dim(top_soft, top_start, top_rows, 2)
    top_dk, top_dv = key_parts(key_grad_cols, key_soft_cols, top_q, top_low_all)
    query_grad = (
        base_dq + place_rows(mid_dq, R1, mid_shift) + place_rows(top_dq, ctx_size, top_shift)
    )
    key_grad = base_dk + place_rows(mid_dk, R1, mid_shift) + place_rows(top_dk, ctx_size, top_shift)
    value_grad = (
        base_dv + place_rows(mid_dv, R1, mid_shift) + place_rows(top_dv, ctx_size, top_shift)
    )
    out_shape = (1, tokens, flat_width)
    return (
        attended,
        query_grad.astype(jnp.bfloat16).reshape(out_shape),
        key_grad.astype(jnp.bfloat16).reshape(out_shape),
        value_grad.astype(jnp.bfloat16).reshape(out_shape),
        gain_grad,
    )


def solution(mesh):
    in_specs = (
        P("dp", "ctx", "head"),
        P("dp", "ctx", "head"),
        P("dp", "ctx", "head"),
        P("dp", "ctx", "head"),
        P("head"),
        P(None, "head"),
    )
    out_specs = (
        P("dp", "ctx", "head"),
        P("dp", "ctx", "head"),
        P("dp", "ctx", "head"),
        P("dp", "ctx", "head"),
        P("head"),
    )
    return jax.shard_map(shards, mesh=mesh, in_specs=in_specs, out_specs=out_specs, check_vma=False)
```

profile of v0, /device:TPU:256, one launch (start us, length us, event | category | flops | bytes accessed | tf_op | source)
XLA Modules:
  0.0 428.5 jit_solution(14037007713612233846)
XLA Ops:
  0.6 0.8 slice_bitcast_fusion.5
  1.4 0.6 copy-done.23
  2.0 1.5 fusion.24
  3.6 5.5 %collective-permute-start.2 = (bf16[16,1920]{1,0:T(8,128)(2,1)S(1)}, bf16[16,1920]{1,0:T(8,128)(2,1)S(1)}, u32[]{:S(2)}, u32[]{:S(2)}) collective-permute-start(bf16[16,1920]{1,0:T(8,128)(2,1)S(1)} %bitcast_dynamic-update-slice_fusion), channel_id=1, source_target_pairs={{0,12},{4,0},{8,4},{12,8},{16,28},{20,16},{24,20},{28,24},{32,44},... | collective-permute-start | bytes 184328 | tf_op jit(solution)/shard_map/ppermute | solution.py:21
  9.1 1.9 collective-permute-start.1
  11.0 2.9 collective-permute-start
  14.1 0.7 copy-done.1
  15.1 0.7 copy-done.2
  16.8 0.4 copy-done.21
  17.2 0.7 broadcast_in_dim.285
  17.9 0.6 broadcast_in_dim.278
  18.9 0.3 select_reduce_fusion.2
  19.2 50.0 %all-gather = bf16[64,2,1920]{2,1,0:T(2,128)(2,1)S(1)} all-gather(bf16[1,2,1920]{2,1,0:T(2,128)(2,1)S(1)} %maximum_bitcast_fusion.1), channel_id=1, replica_groups=mesh['dp'=2,'ctx'=64,'head'=4] {'ctx'}, dimensions={0}, use_global_device_ids=true | all-gather | bytes 499200 | tf_op jit(solution)/shard_map/all_gather | solution.py:125
  69.9 0.3 fusion.67
  70.4 0.5 copy-done.7
  71.0 0.7 broadcast_in_dim.289
  72.0 0.3 fusion.69
  72.8 0.5 copy-done.9
  73.8 0.4 copy-done.19
  74.9 0.5 multiply_reduce_fusion.3
  75.5 0.7 copy-done.13
  76.1 0.8 multiply_reduce_fusion
  76.9 0.7 copy-done.15
  78.0 0.6 negate_bitcast_fusion
  79.1 0.6 pad_maximum_fusion.2
  79.7 2.6 collective-permute-start.5
  82.3 3.1 collective-permute-start.4
  85.4 2.3 collective-permute-start.3
  88.0 0.4 copy-done.22
  88.7 49.2 %all-gather.1 = f32[64,2,645]{2,1,0:T(2,128)S(1)} all-gather(f32[1,2,645]{2,1,0:T(2,128)S(1)} %maximum_bitcast_fusion.2), channel_id=1, replica_groups=mesh['dp'=2,'ctx'=64,'head'=4] {'ctx'}, dimensions={0}, use_global_device_ids=true | all-gather | bytes 335400 | tf_op jit(solution)/shard_map/all_gather | solution.py:179
  137.9 0.3 reshape.372
  138.2 0.7 slice.99
  138.9 0.4 fusion.17
  139.3 0.5 copy-done.3
  140.1 0.5 copy-done.8
  141.1 0.4 convolution_bitcast_fusion.8
  141.7 0.8 copy.357
  142.7 0.5 copy-done.17
  143.2 277.9 %psum.7 = f32[640]{0:T(1024)} all-reduce(f32[640]{0:T(1024)S(1)} %bitcast.273), channel_id=1, replica_groups=mesh['dp'=2,'ctx'=64,'head'=4] {'dp','ctx'}, use_global_device_ids=true, to_apply=%region_22.23 | all-reduce | flops 640 | bytes 5120 | tf_op jit(solution)/shard_map/psum | solution.py:158
  421.1 0.9 pad_maximum_fusion.1
  422.1 0.8 maximum_bitcast_fusion
  423.0 0.5 copy-done.10
  424.1 0.6 copy-done.12
  425.1 0.8 copy.359
  426.0 0.3 fusion.13
  426.4 0.8 copy.358
  427.2 0.3 fusion.15
  427.7 0.8 copy.360
  (128 shorter events, 8.9 us)
Async XLA Ops:
  1.4 0.6 copy-start.23
  1.4 15.2 %copy-start.25 = (s32[5]{0:T(128)}, s32[5]{0:T(128)S(1)}, u32[]{:S(2)}) copy-start(s32[5]{0:T(128)S(1)} %get-tuple-element.62) | copy-start | bytes 64
  2.0 15.9 %copy-start.14 = (pred[8,5]{0,1:T(8,128)(4,1)}, pred[8,5]{0,1:T(8,128)(4,1)S(1)}, u32[]{:S(2)}) copy-start(pred[8,5]{0,1:T(8,128)(4,1)S(1)} %iota_compare_fusion.1) | copy-start | bytes 124
  2.0 11.9 %copy-start = (bf16[1,128,640]{2,1,0:T(8,128)(2,1)S(1)}, bf16[1,128,640]{2,1,0:T(8,128)(2,1)}, u32[]{:S(2)}) copy-start(bf16[1,128,640]{2,1,0:T(8,128)(2,1)} %param.6) | copy-start | bytes 491524
  3.6 68.8 %collective-permute-start.2 = (bf16[16,1920]{1,0:T(8,128)(2,1)S(1)}, bf16[16,1920]{1,0:T(8,128)(2,1)S(1)}, u32[]{:S(2)}, u32[]{:S(2)}) collective-permute-start(bf16[16,1920]{1,0:T(8,128)(2,1)S(1)} %bitcast_dynamic-update-slice_fusion), channel_id=1, source_target_pairs={{0,12},{4,0},{8,4},{12,8},{16,28},{20,16},{24,20},{28,24},{32,44},... | collective-permute-start | bytes 184328 | tf_op jit(solution)/shard_map/ppermute | solution.py:21
  9.1 63.3 %collective-permute-start.1 = (bf16[16,1920]{1,0:T(8,128)(2,1)S(1)}, bf16[16,1920]{1,0:T(8,128)(2,1)S(1)}, u32[]{:S(2)}, u32[]{:S(2)}) collective-permute-start(bf16[16,1920]{1,0:T(8,128)(2,1)S(1)} %bitcast_dynamic-update-slice_fusion), channel_id=1, source_target_pairs={{0,8},{4,12},{8,0},{12,4},{16,24},{20,28},{24,16},{28,20},{32,40},... | collective-permute-start | bytes 184328 | tf_op jit(solution)/shard_map/ppermute | solution.py:21
  11.0 61.3 %collective-permute-start = (bf16[16,1920]{1,0:T(8,128)(2,1)S(1)}, bf16[16,1920]{1,0:T(8,128)(2,1)S(1)}, u32[]{:S(2)}, u32[]{:S(2)}) collective-permute-start(bf16[16,1920]{1,0:T(8,128)(2,1)S(1)} %bitcast_dynamic-update-slice_fusion), channel_id=1, source_target_pairs={{0,4},{4,8},{8,12},{12,0},{16,20},{20,24},{24,28},{28,16},{32,36},... | collective-permute-start | bytes 184328 | tf_op jit(solution)/shard_map/ppermute | solution.py:21
  14.0 0.9 copy-start.1
  14.9 0.9 copy-start.2
  16.4 2.2 copy-start.6
  16.7 0.5 copy-start.21
  70.3 0.6 copy-start.7
  72.4 1.0 copy-start.4
  72.7 0.6 copy-start.9
  73.5 0.7 copy-start.19
  73.5 0.7 copy-start.26
  73.7 0.7 copy-start.18
  73.7 0.7 copy-start.11
  73.8 0.7 copy-start.24
  75.4 0.7 copy-start.13
  76.9 0.7 copy-start.15
  79.7 341.3 %collective-permute-start.5 = (f32[16,645]{1,0:T(8,128)}, f32[16,645]{1,0:T(8,128)}, u32[]{:S(2)}, u32[]{:S(2)}) collective-permute-start(f32[16,645]{1,0:T(8,128)} %pad_maximum_fusion.2), channel_id=1, source_target_pairs={{0,12},{4,0},{8,4},{12,8},{16,28},{20,16},{24,20},{28,24},{32,44},... | collective-permute-start | bytes 123848 | tf_op jit(solution)/shard_map/ppermute | solution.py:21
  82.3 338.8 %collective-permute-start.4 = (f32[16,645]{1,0:T(8,128)}, f32[16,645]{1,0:T(8,128)}, u32[]{:S(2)}, u32[]{:S(2)}) collective-permute-start(f32[16,645]{1,0:T(8,128)} %pad_maximum_fusion.2), channel_id=1, source_target_pairs={{0,8},{4,12},{8,0},{12,4},{16,24},{20,28},{24,16},{28,20},{32,40},... | collective-permute-start | bytes 123848 | tf_op jit(solution)/shard_map/ppermute | solution.py:21
  85.4 335.7 %collective-permute-start.3 = (f32[16,645]{1,0:T(8,128)}, f32[16,645]{1,0:T(8,128)}, u32[]{:S(2)}, u32[]{:S(2)}) collective-permute-start(f32[16,645]{1,0:T(8,128)} %pad_maximum_fusion.2), channel_id=1, source_target_pairs={{0,4},{4,8},{8,12},{12,0},{16,20},{20,24},{24,28},{28,16},{32,36},... | collective-permute-start | bytes 123848 | tf_op jit(solution)/shard_map/ppermute | solution.py:21
  87.7 0.6 copy-start.22
  138.2 0.7 copy-start.16
  138.9 0.9 copy-start.3
  140.0 0.7 copy-start.8
  141.7 0.8 copy-start.20
  142.5 0.7 copy-start.17
  422.1 0.9 copy-start.5
  422.8 0.7 copy-start.10
  424.1 0.6 copy-start.12
where the time goes:
time: 429 us
  blocking collectives  377 us (88%)
  local copies, waits for them, and re-layouts  19.9 us (5%)
  starting transfers between devices  18.3 us (4%)
  other arithmetic  7.42 us (2%)
  matrix products  4.56 us (1%)
    psum x1, blocking collectives, shards(): gain_grad = lax.psum(gain_part, ('dp', 'ctx'))  278 us
    all_gather x1, blocking collectives, shards(): top_all = lax.all_gather(top_pack, 'ctx', axis=0, tiled=True)  50 us
    all_gather x1, blocking collectives, shards(): lax.all_gather(pack_grads(top_low, top_row_shift), 'ctx', axis=0, tiled=T...  49.2 us
    ppermute x6, starting transfers between devices, group_gather(): pieces.append(lax.ppermute(block, axis, route))  18.3 us
    unnamed x69, local copies, waits for them, and re-layouts  13.1 us
  transfers between devices with their start and end apart: 6, of which 0 were waited for; matrix products, arithmetic and copies ran while one was open for 2% of the time, Pallas kernels for 0%

commit v1 on v0

--- a/solution.py
+++ b/solution.py
@@ -155,7 +155,7 @@
     attended = (normed * gain_rows).astype(jnp.bfloat16).reshape(1, tokens, flat_width)
     grad_full = grad_y[0].reshape(row_shape).astype(jnp.float32)
     gain_part = jnp.sum(grad_full * normed, axis=0).reshape(flat_width)
-    gain_grad = lax.psum(gain_part, ("dp", "ctx"))
+    gain_grad = lax.psum(lax.psum(gain_part, "dp"), "ctx")
     grad_norm = grad_full * gain_rows
     grad_attn = inv_rms * (
         grad_norm - normed * jnp.mean(grad_norm * normed, axis=-1, keepdims=True)

time: 429 us -> 303 us (0.71)
  the two profiles are of different devices: /device:TPU:256 before, /device:TPU:4 now
where the time goes in v1:
time: 303 us; the launch traced here: 302 us
  blocking collectives  250 us (83%)
  local copies, waits for them, and re-layouts  19.9 us (7%)
  starting transfers between devices  18.9 us (6%)
  other arithmetic  7.42 us (2%)
  matrix products  4.56 us (2%)
    psum x2, blocking collectives, shards(): gain_grad = lax.psum(lax.psum(gain_part, 'dp'), 'ctx')  144 us
    all_gather x1, blocking collectives, shards(): top_all = lax.all_gather(top_pack, 'ctx', axis=0, tiled=True)  56.5 us
    all_gather x1, blocking collectives, shards(): lax.all_gather(pack_grads(top_low, top_row_shift), 'ctx', axis=0, tiled=T...  49.6 us
    ppermute x6, starting transfers between devices, group_gather(): pieces.append(lax.ppermute(block, axis, route))  18.9 us
    unnamed x69, local copies, waits for them, and re-layouts  13.1 us
  transfers between devices with their start and end apart: 6, of which 0 were waited for; matrix products, arithmetic and copies ran while one was open for 3% of the time, Pallas kernels for 0%

profile of v1, /device:TPU:4, one launch (start us, length us, event | category | flops | bytes accessed | tf_op | source)
XLA Modules:
  0.0 301.9 jit_solution(9746207625792519524)
XLA Ops:
  0.6 0.8 slice_bitcast_fusion.5
  1.4 0.6 copy-done.23
  2.0 1.5 fusion.24
  3.6 5.5 %collective-permute-start.2 = (bf16[16,1920]{1,0:T(8,128)(2,1)S(1)}, bf16[16,1920]{1,0:T(8,128)(2,1)S(1)}, u32[]{:S(2)}, u32[]{:S(2)}) collective-permute-start(bf16[16,1920]{1,0:T(8,128)(2,1)S(1)} %bitcast_dynamic-update-slice_fusion), channel_id=1, source_target_pairs={{0,12},{4,0},{8,4},{12,8},{16,28},{20,16},{24,20},{28,24},{32,44},... | collective-permute-start | bytes 184328 | tf_op jit(solution)/shard_map/ppermute | solution.py:21
  9.1 1.9 collective-permute-start.1
  11.0 2.9 collective-permute-start
  14.1 0.7 copy-done.1
  15.1 0.7 copy-done.2
  16.8 0.4 copy-done.21
  17.2 0.7 broadcast_in_dim.285
  17.9 0.6 broadcast_in_dim.278
  18.9 0.3 select_reduce_fusion.2
  19.2 56.5 %all-gather = bf16[64,2,1920]{2,1,0:T(2,128)(2,1)S(1)} all-gather(bf16[1,2,1920]{2,1,0:T(2,128)(2,1)S(1)} %maximum_bitcast_fusion.1), channel_id=1, replica_groups=mesh['dp'=2,'ctx'=64,'head'=4] {'ctx'}, dimensions={0}, use_global_device_ids=true | all-gather | bytes 499200 | tf_op jit(solution)/shard_map/all_gather | solution.py:125
  76.4 0.3 fusion.67
  76.9 0.5 copy-done.7
  77.5 0.7 broadcast_in_dim.289
  78.5 0.3 fusion.69
  79.3 0.5 copy-done.9
  80.3 0.4 copy-done.19
  81.4 0.5 multiply_reduce_fusion.3
  82.0 0.7 copy-done.13
  82.6 0.8 multiply_reduce_fusion
  83.4 0.7 copy-done.15
  84.5 0.6 negate_bitcast_fusion
  85.6 0.6 pad_maximum_fusion.2
  86.2 3.6 %collective-permute-start.5 = (f32[16,645]{1,0:T(8,128)}, f32[16,645]{1,0:T(8,128)}, u32[]{:S(2)}, u32[]{:S(2)}) collective-permute-start(f32[16,645]{1,0:T(8,128)} %pad_maximum_fusion.2), channel_id=1, source_target_pairs={{0,12},{4,0},{8,4},{12,8},{16,28},{20,16},{24,20},{28,24},{32,44},... | collective-permute-start | bytes 123848 | tf_op jit(solution)/shard_map/ppermute | solution.py:21
  89.8 3.1 %collective-permute-start.4 = (f32[16,645]{1,0:T(8,128)}, f32[16,645]{1,0:T(8,128)}, u32[]{:S(2)}, u32[]{:S(2)}) collective-permute-start(f32[16,645]{1,0:T(8,128)} %pad_maximum_fusion.2), channel_id=1, source_target_pairs={{0,8},{4,12},{8,0},{12,4},{16,24},{20,28},{24,16},{28,20},{32,40},... | collective-permute-start | bytes 123848 | tf_op jit(solution)/shard_map/ppermute | solution.py:21
  92.9 1.9 collective-permute-start.3
  95.1 0.4 copy-done.22
  95.8 49.6 %all-gather.1 = f32[64,2,645]{2,1,0:T(2,128)S(1)} all-gather(f32[1,2,645]{2,1,0:T(2,128)S(1)} %maximum_bitcast_fusion.2), channel_id=1, replica_groups=mesh['dp'=2,'ctx'=64,'head'=4] {'ctx'}, dimensions={0}, use_global_device_ids=true | all-gather | bytes 335400 | tf_op jit(solution)/shard_map/all_gather | solution.py:179
  145.4 0.3 reshape.372
  145.7 0.7 slice.99
  146.4 0.4 fusion.17
  146.9 0.5 copy-done.3
  147.7 0.5 copy-done.8
  148.7 0.4 convolution_bitcast_fusion.8
  149.2 0.8 copy.357
  150.2 0.5 copy-done.17
  150.7 2.4 psum.14
  153.2 141.2 %psum.15 = f32[640]{0:T(1024)} all-reduce(f32[640]{0:T(1024)S(1)} %psum.14), channel_id=1, replica_groups=mesh['dp'=2,'ctx'=64,'head'=4] {'ctx'}, use_global_device_ids=true, to_apply=%region_23.24 | all-reduce | flops 640 | bytes 5120 | tf_op jit(solution)/shard_map/psum | solution.py:158
  294.4 0.9 pad_maximum_fusion.1
  295.4 0.8 maximum_bitcast_fusion
  296.4 0.5 copy-done.10
  297.4 0.6 copy-done.12
  298.5 0.8 copy.359
  299.7 0.8 copy.358
  300.6 0.3 fusion.15
  301.0 0.8 copy.360
  (129 shorter events, 9.1 us)
Async XLA Ops:
  1.4 0.6 copy-start.23
  1.4 15.2 %copy-start.25 = (s32[5]{0:T(128)}, s32[5]{0:T(128)S(1)}, u32[]{:S(2)}) copy-start(s32[5]{0:T(128)S(1)} %get-tuple-element.62) | copy-start | bytes 64
  2.0 15.9 %copy-start.14 = (pred[8,5]{0,1:T(8,128)(4,1)}, pred[8,5]{0,1:T(8,128)(4,1)S(1)}, u32[]{:S(2)}) copy-start(pred[8,5]{0,1:T(8,128)(4,1)S(1)} %iota_compare_fusion.1) | copy-start | bytes 124
  2.0 11.9 %copy-start = (bf16[1,128,640]{2,1,0:T(8,128)(2,1)S(1)}, bf16[1,128,640]{2,1,0:T(8,128)(2,1)}, u32[]{:S(2)}) copy-start(bf16[1,128,640]{2,1,0:T(8,128)(2,1)} %param.6) | copy-start | bytes 491524
  3.6 75.3 %collective-permute-start.2 = (bf16[16,1920]{1,0:T(8,128)(2,1)S(1)}, bf16[16,1920]{1,0:T(8,128)(2,1)S(1)}, u32[]{:S(2)}, u32[]{:S(2)}) collective-permute-start(bf16[16,1920]{1,0:T(8,128)(2,1)S(1)} %bitcast_dynamic-update-slice_fusion), channel_id=1, source_target_pairs={{0,12},{4,0},{8,4},{12,8},{16,28},{20,16},{24,20},{28,24},{32,44},... | collective-permute-start | bytes 184328 | tf_op jit(solution)/shard_map/ppermute | solution.py:21
  9.1 69.8 %collective-permute-start.1 = (bf16[16,1920]{1,0:T(8,128)(2,1)S(1)}, bf16[16,1920]{1,0:T(8,128)(2,1)S(1)}, u32[]{:S(2)}, u32[]{:S(2)}) collective-permute-start(bf16[16,1920]{1,0:T(8,128)(2,1)S(1)} %bitcast_dynamic-update-slice_fusion), channel_id=1, source_target_pairs={{0,8},{4,12},{8,0},{12,4},{16,24},{20,28},{24,16},{28,20},{32,40},... | collective-permute-start | bytes 184328 | tf_op jit(solution)/shard_map/ppermute | solution.py:21
  11.0 67.8 %collective-permute-start = (bf16[16,1920]{1,0:T(8,128)(2,1)S(1)}, bf16[16,1920]{1,0:T(8,128)(2,1)S(1)}, u32[]{:S(2)}, u32[]{:S(2)}) collective-permute-start(bf16[16,1920]{1,0:T(8,128)(2,1)S(1)} %bitcast_dynamic-update-slice_fusion), channel_id=1, source_target_pairs={{0,4},{4,8},{8,12},{12,0},{16,20},{20,24},{24,28},{28,16},{32,36},... | collective-permute-start | bytes 184328 | tf_op jit(solution)/shard_map/ppermute | solution.py:21
  14.0 0.9 copy-start.1
  14.9 0.9 copy-start.2
  16.4 2.2 copy-start.6
  16.7 0.5 copy-start.21
  76.8 0.6 copy-start.7
  78.9 1.0 copy-start.4
  79.2 0.6 copy-start.9
  80.0 0.7 copy-start.19
  80.0 0.7 copy-start.26
  80.2 0.7 copy-start.18
  80.2 0.7 copy-start.11
  80.3 0.7 copy-start.24
  82.0 0.7 copy-start.13
  83.4 0.7 copy-start.15
  86.2 208.2 %collective-permute-start.5 = (f32[16,645]{1,0:T(8,128)}, f32[16,645]{1,0:T(8,128)}, u32[]{:S(2)}, u32[]{:S(2)}) collective-permute-start(f32[16,645]{1,0:T(8,128)} %pad_maximum_fusion.2), channel_id=1, source_target_pairs={{0,12},{4,0},{8,4},{12,8},{16,28},{20,16},{24,20},{28,24},{32,44},... | collective-permute-start | bytes 123848 | tf_op jit(solution)/shard_map/ppermute | solution.py:21
  89.8 204.6 %collective-permute-start.4 = (f32[16,645]{1,0:T(8,128)}, f32[16,645]{1,0:T(8,128)}, u32[]{:S(2)}, u32[]{:S(2)}) collective-permute-start(f32[16,645]{1,0:T(8,128)} %pad_maximum_fusion.2), channel_id=1, source_target_pairs={{0,8},{4,12},{8,0},{12,4},{16,24},{20,28},{24,16},{28,20},{32,40},... | collective-permute-start | bytes 123848 | tf_op jit(solution)/shard_map/ppermute | solution.py:21
  92.9 201.5 %collective-permute-start.3 = (f32[16,645]{1,0:T(8,128)}, f32[16,645]{1,0:T(8,128)}, u32[]{:S(2)}, u32[]{:S(2)}) collective-permute-start(f32[16,645]{1,0:T(8,128)} %pad_maximum_fusion.2), channel_id=1, source_target_pairs={{0,4},{4,8},{8,12},{12,0},{16,20},{20,24},{24,28},{28,16},{32,36},... | collective-permute-start | bytes 123848 | tf_op jit(solution)/shard_map/ppermute | solution.py:21
  94.8 0.6 copy-start.22
  145.7 0.7 copy-start.16
  146.4 0.9 copy-start.3
  147.5 0.7 copy-start.8
  149.2 0.8 copy-start.20
  150.1 0.7 copy-start.17
  295.4 0.9 copy-start.5
  296.2 0.7 copy-start.10
  297.4 0.6 copy-start.12
